TPU v7x, 32 devices: a whole 2x2x4 slice. The times are simulated.
32 devices in a mesh: groups: 2 (over y), chol: 4 (over z), walk: 4 (over x, core).
Axes of the slice: x: 2, y: 2, z: 4, core: 2. Of those that a mesh axis runs over, the one named last changes fastest.
Arguments:
- green: bfloat16 [8, 200, 1600], P(('groups', 'walk')), parts along dimension 0, may hold values from -2 to 2
- chol: bfloat16 [16, 200, 1600], P(('groups', 'chol')), parts along dimension 0, may hold values from -0.19921875 to 0.19921875
- trial: bfloat16 [3200, 200], P(('groups', 'chol')), parts along dimension 0, may hold values from -1.1953125 to 1.1953125
- hamil: bfloat16 [1600, 1600], P('chol'), may hold values from -0.21875 to 0.21875
- energy_cot: float32 [8], P('groups'), parts along dimension 0, may hold values from -4 to 4
Outputs:
- d_green: float32 [8, 200, 1600], P(('groups', 'walk'), None, 'chol'), parts along dimension 0
- d_chol: float32 [16, 200, 1600], P(('groups', 'chol'), None, 'walk'), parts along dimension 0
- d_trial: float32 [3200, 200], P(('groups', 'chol')), parts along dimension 0
There are 2 independent parts, one for each index of `groups`. A program takes and returns all parts, laid end to end along the dimension named above; an argument that names none is the same for every part. Nothing has to cross between parts.
All inputs are finite; a program needn't handle non-finite values.
Results may differ from a plain program's by a relative error of at most 0.0029.
Values may be sent and summed in bfloat16 or wider, within the bound.
No kernel may reach another device: no remote copies, remote signals or barrier semaphores. Data moves between devices by JAX's collectives and lax.ppermute only.
A program may use at most 64 MiB of HBM per device.

v0:
```python
import jax
import jax.numpy as jnp
from jax import lax
from jax.sharding import PartitionSpec as P


def shards(green, chol, trial, hamil, energy_cot):
    walk_rank = lax.axis_index("walk")
    walk_rows = green.shape[0]
    cot_own = lax.dynamic_slice_in_dim(energy_cot, walk_rank * walk_rows, walk_rows, 0)
    hrot_part = lax.dot_general(
        trial, hamil, (((0,), (0,)), ((), ())), preferred_element_type=jnp.float32
    )
    identity = jnp.eye(trial.shape[1], dtype=jnp.float32)
    quarter = green.shape[2] // lax.axis_size("walk")
    greens = lax.all_gather(green, "walk", axis=0, tiled=True)
    coulomb = jnp.einsum("cip,wip->cw", chol, greens, preferred_element_type=jnp.float32)
    exchange_mat = jnp.einsum("cip,wjp->cwij", chol, greens, preferred_element_type=jnp.float32)
    kernel_mat = (
        energy_cot[None, :, None, None] * (coulomb[:, :, None, None] * identity - exchange_mat)
    ).astype(jnp.bfloat16)
    kernel_own = lax.dynamic_slice_in_dim(kernel_mat, walk_rank * walk_rows, walk_rows, 1)
    green_part = jnp.einsum("cwij,cjp->wip", kernel_own, chol, preferred_element_type=jnp.float32)
    green_part = green_part + cot_own[:, None, None] * hrot_part[None]
    d_green = lax.psum_scatter(green_part, "chol", scatter_dimension=2, tiled=True)
    green_share = lax.dynamic_slice_in_dim(greens, walk_rank * quarter, quarter, 2)
    d_chol = jnp.einsum(
        "cwji,wjp->cip", kernel_mat, green_share, preferred_element_type=jnp.float32
    )
    gbar = jnp.einsum(
        "w,wip->ip",
        energy_cot,
        greens,
        precision=lax.Precision.HIGHEST,
        preferred_element_type=jnp.float32,
    ).astype(jnp.bfloat16)
    d_trial = lax.dot_general(
        hamil, gbar, (((1,), (1,)), ((), ())), preferred_element_type=jnp.float32
    )
    return (d_green, d_chol, d_trial)


def solution(mesh):
    return jax.shard_map(
        shards,
        mesh=mesh,
        in_specs=(
            P(("groups", "walk"), None, None),
            P(("groups", "chol"), None, None),
            P(("groups", "chol"), None),
            P("chol", None),
            P("groups"),
        ),
        out_specs=(
            P(("groups", "walk"), None, "chol"),
            P(("groups", "chol"), None, "walk"),
            P(("groups", "chol"), None),
        ),
        check_vma=False,
    )
```

profile of v0, /device:TPU:0, one launch (start us, length us, event | category | flops | bytes accessed | tf_op | source)
XLA Modules:
  0.0 101.0 jit_solution(4208986423430562566)
XLA Ops:
  7.2 0.0 copy-start
  7.2 0.0 all-gather.2.cloned.1.call-start
  7.2 0.7 all-gather.2.cloned.1.call-update
  7.9 0.0 reduce-scatter.4.cloned.1.call-start
  8.0 1.2 %dynamic_slice.10 = f32[1]{0:T(128)} dynamic-slice(f32[4]{0:T(128)} %param.9, s32[]{:T(128)S(6)} %select_n.7), dynamic_slice_sizes={1} | dynamic-slice | bytes 12 | tf_op jit(solution)/shard_map/dynamic_slice | solution.py:10
  9.2 0.0 copy-start.1
  9.2 0.0 copy-start.6
  9.2 28.8 %all-gather.2.cloned.1.call-done = bf16[4,200,1600]{2,1,0:T(8,128)(2,1)} async-done(((bf16[1,200,1600]{2,1,0:T(8,128)(2,1)}), bf16[4,200,1600]{2,1,0:T(8,128)(2,1)}) %all-gather.2.cloned.1.call-update) | async-done | bytes 2560016 | tf_op jit(solution)/shard_map/all_gather | solution.py:16
  38.1 0.0 copy-start.5
  38.1 5.9 %fusion.14 = f32[2,4]{0,1:T(4,128)S(1)} fusion(bf16[4,200,1600]{2,1,0:T(8,128)(2,1)} %all-gather.2.cloned.1.call-done, bf16[2,200,1600]{2,1,0:T(8,128)(2,1)} %param.6), kind=kOutput, calls=%fused_computation.19 | convolution fusion | flops 5120000 | bytes 3840032 | tf_op jit(solution)/shard_map/cip,wip->cw/dot_general | solution.py:17
  44.0 0.0 copy-done.1
  44.0 0.0 copy-done.6
  44.0 0.0 copy-done.5
  44.0 1.7 %fusion.9 = bf16[2,4,200,200]{2,3,0,1:T(8,128)(2,1)S(1)} fusion(bf16[4,200,1600]{2,1,0:T(8,128)(2,1)S(1)} %copy-done.5, bf16[2,200,1600]{2,1,0:T(8,128)(2,1)S(1)} %copy-done.1, f32[200,200]{0,1:T(8,128)S(1)} %fusion.23, f32[2,4]{0,1:T(4,128)S(1)} %fusion.14, f32[4]{0:T(128)S(1)} %copy-done.6), kind=kOutput, calls=%fused_computation.13 | convolution fusion | flops 1025280000 | bytes 4640048 | tf_op jit(solution)/shard_map/cip,wjp->cwij/dot_general | solution.py:18
  45.7 0.0 copy-start.3
  45.7 0.0 copy-start.2
  45.7 0.6 convolution_bitcast_fusion
  46.3 0.3 copy-done.3
  46.6 0.0 copy-done
  46.6 0.3 copy-done.2
  46.9 2.3 %fusion.3 = f32[1,200,1600]{2,1,0:T(8,128)} fusion(f32[200,1600]{1,0:T(8,128)S(1)} %convolution_bitcast_fusion, bf16[400,200]{1,0:T(8,128)(2,1)S(1)} %copy-done.2, bf16[400,1600]{1,0:T(8,128)(2,1)S(1)} %copy-done, f32[]{:T(128)} %bitcast.7), kind=kOutput, calls=%fused_computation.5 | convolution fusion | flops 256640000 | bytes 4000004 | tf_op jit(solution)/shard_map/dot_general | solution.py:11
  49.1 4.6 %copy.33 = f32[1,200,1600]{1,0,2:T(1,128)S(1)} copy(f32[1,200,1600]{2,1,0:T(8,128)} %fusion.3) | data formatting | bytes 2560000
  53.8 1.3 %copy.49 = f32[1600,1,200]{2,0,1:T(8,128)} copy(f32[1600,1,200]{2,1,0:T(1,128)S(1)} %bitcast.54) | data formatting | bytes 2560000
  55.0 0.0 reduce-scatter.4.cloned.1.call-update
  55.1 6.2 %fusion.4 = bf16[1,200,1600]{2,0,1:T(2,128)(2,1)S(1)} fusion(bf16[4,200,1600]{2,1,0:T(8,128)(2,1)} %all-gather.2.cloned.1.call-done, f32[4]{0:T(128)S(1)} %copy-done.6), kind=kOutput, calls=%fused_computation.6 | convolution fusion | flops 15360000 | bytes 3200016 | tf_op jit(solution)/shard_map/w,wip->ip/dot_general | solution.py:30
  61.3 0.0 copy-start.4
  61.3 0.6 convolution_bitcast_fusion.2
  61.9 0.9 copy.27
  62.8 0.0 copy-done.4
  62.8 2.8 %convolution_bitcast_fusion.1 = f32[2,200,400]{2,1,0:T(8,128)} fusion(bf16[2,4,200,200]{2,3,0,1:T(8,128)(2,1)S(1)} %copy-done.4, bf16[4,200,1600]{2,1,0:T(8,128)(2,1)} %all-gather.2.cloned.1.call-done, s32[]{:T(128)S(6)} %select_n.8), kind=kOutput, calls=%fused_computation.17 | convolution fusion | flops 256000000 | bytes 2099204 | tf_op jit(solution)/shard_map/cwji,wjp->cip/dot_general | solution.py:27
  65.6 26.0 %reduce-scatter.4.cloned.1.call-done = f32[400,200]{1,0:T(8,128)} async-done(((f32[1600,200]{1,0:T(8,128)}), f32[400,200]{1,0:T(8,128)}) %reduce-scatter.4.cloned.1.call-update) | async-done | bytes 320016
  91.7 1.3 %reshape_bitcast_fusion = f32[1,200,400]{1,0,2:T(1,128)S(1)} fusion(f32[400,200]{1,0:T(8,128)} %reduce-scatter.4.cloned.1.call-done), kind=kLoop, calls=%fused_computation.22 | loop fusion | bytes 640000
  93.0 1.2 %copy.34 = f32[1,200,400]{2,1,0:T(8,128)} copy(f32[1,200,400]{1,0,2:T(1,128)S(1)} %reshape_bitcast_fusion) | data formatting | bytes 640000
  (1 shorter events, 0.0 us)
Async XLA Ops:
  7.2 39.4 %copy-start = (bf16[400,1600]{1,0:T(8,128)(2,1)S(1)}, bf16[400,1600]{1,0:T(8,128)(2,1)}, u32[]{:S(2)}) copy-start(bf16[400,1600]{1,0:T(8,128)(2,1)} %param.8) | copy-start | bytes 3840004
  7.2 30.9 %all-gather.2.cloned.1.call-start = ((), (), s32[]{:S(2)}) async-start(), calls=%async_computation.1 | async-start | bytes 3328000 | tf_op jit(solution)/shard_map/all_gather | solution.py:16
  7.9 83.8 %reduce-scatter.4.cloned.1.call-start = ((), (), s32[]{:S(2)}) async-start(), calls=%async_computation.2 | async-start | bytes 2048000
  9.2 34.7 %copy-start.1 = (bf16[2,200,1600]{2,1,0:T(8,128)(2,1)S(1)}, bf16[2,200,1600]{2,1,0:T(8,128)(2,1)}, u32[]{:S(2)}) copy-start(bf16[2,200,1600]{2,1,0:T(8,128)(2,1)} %param.6) | copy-start | bytes 3840004
  9.2 34.7 %copy-start.6 = (f32[4]{0:T(128)S(1)}, f32[4]{0:T(128)}, u32[]{:S(2)}) copy-start(f32[4]{0:T(128)} %param.9) | copy-start | bytes 52
  38.1 5.9 %copy-start.5 = (bf16[4,200,1600]{2,1,0:T(8,128)(2,1)S(1)}, bf16[4,200,1600]{2,1,0:T(8,128)(2,1)}, u32[]{:S(2)}) copy-start(bf16[4,200,1600]{2,1,0:T(8,128)(2,1)} %all-gather.2.cloned.1.call-done) | copy-start | bytes 7680004
  45.7 0.9 copy-start.3
  45.7 1.2 %copy-start.2 = (bf16[400,200]{1,0:T(8,128)(2,1)S(1)}, bf16[400,200]{1,0:T(8,128)(2,1)}, u32[]{:S(2)}) copy-start(bf16[400,200]{1,0:T(8,128)(2,1)} %param.7) | copy-start | bytes 480004
  61.3 1.5 %copy-start.4 = (bf16[2,4,200,200]{2,3,0,1:T(8,128)(2,1)S(1)}, bf16[2,4,200,200]{2,3,0,1:T(8,128)(2,1)}, u32[]{:S(2)}) copy-start(bf16[2,4,200,200]{2,3,0,1:T(8,128)(2,1)} %copy-done.3) | copy-start | bytes 1920004
Sparse Core Ops, SparseCore 0:
  9.5 28.4 all-gather.1
  55.2 36.4 reduce-scatter.3
where the time goes:
time: 101 us
  waiting for transfers between devices  55.6 us (55%)
  matrix products  20 us (20%)
  between operations  14.1 us (14%)
  local copies, waits for them, and re-layouts  11.2 us (11%)
    all_gather x1, waiting for transfers between devices, shards(): greens = lax.all_gather(green, 'walk', axis=0, tiled=True)  28.8 us
    unnamed x3, waiting for transfers between devices  26.7 us
    unnamed x19, local copies, waits for them, and re-layouts  9.96 us
    dot_general x1, matrix products, shards(): jnp.einsum('w,wip->ip', energy_cot, greens, precision=lax.Precision.HIGHE...  6.17 us
    dot_general x1, matrix products, shards(): jnp.einsum('cip,wip->cw', chol, greens, preferred_element_type=jnp.float32)  5.9 us
    dot_general x1, matrix products, shards(): jnp.einsum('cwji,wjp->cip', kernel_mat, green_share, preferred_element_ty...  2.85 us
    dot_general x1, matrix products, shards(): lax.dot_general(trial, hamil, (((0,), (0,)), ((), ())), preferred_element...  2.28 us
  transfers between devices with their start and end apart: 2, of which 2 were waited for; matrix products, arithmetic and copies ran while one was open for 12% of the time, Pallas kernels for 0%

commit v1 on v0

v1 whole, which is shorter than its diff:
```python
import functools

import jax
import jax.numpy as jnp
from jax import lax
from jax.experimental import pallas as pl
from jax.experimental.pallas import tpu as pltpu
from jax.sharding import PartitionSpec as P


F32 = jnp.float32
BF16 = jnp.bfloat16
LANES = 128
SUBLANES = 8
MIB = 1024 * 1024


def plain(green, chol, trial, hamil, energy_cot):
    walk_rank = lax.axis_index("walk")
    walk_rows = green.shape[0]
    cot_own = lax.dynamic_slice_in_dim(energy_cot, walk_rank * walk_rows, walk_rows, 0)
    hrot_part = lax.dot_general(
        trial, hamil, (((0,), (0,)), ((), ())), preferred_element_type=F32
    )
    identity = jnp.eye(trial.shape[1], dtype=F32)
    quarter = green.shape[2] // lax.axis_size("walk")
    greens = lax.all_gather(green, "walk", axis=0, tiled=True)
    coulomb = jnp.einsum("cip,wip->cw", chol, greens, preferred_element_type=F32)
    exchange_mat = jnp.einsum("cip,wjp->cwij", chol, greens, preferred_element_type=F32)
    kernel_mat = (
        energy_cot[None, :, None, None] * (coulomb[:, :, None, None] * identity - exchange_mat)
    ).astype(BF16)
    kernel_own = lax.dynamic_slice_in_dim(kernel_mat, walk_rank * walk_rows, walk_rows, 1)
    green_part = jnp.einsum("cwij,cjp->wip", kernel_own, chol, preferred_element_type=F32)
    green_part = green_part + cot_own[:, None, None] * hrot_part[None]
    d_green = lax.psum_scatter(green_part, "chol", scatter_dimension=2, tiled=True)
    green_share = lax.dynamic_slice_in_dim(greens, walk_rank * quarter, quarter, 2)
    d_chol = jnp.einsum("cwji,wjp->cip", kernel_mat, green_share, preferred_element_type=F32)
    gbar = jnp.einsum(
        "w,wip->ip",
        energy_cot,
        greens,
        precision=lax.Precision.HIGHEST,
        preferred_element_type=F32,
    ).astype(BF16)
    d_trial = lax.dot_general(hamil, gbar, (((1,), (1,)), ((), ())), preferred_element_type=F32)
    return (d_green, d_chol, d_trial)


def nn(a, b):
    return jnp.dot(a, b, preferred_element_type=F32)


def nt(a, b):
    return lax.dot_general(a, b, (((1,), (1,)), ((), ())), preferred_element_type=F32)


def kernel_of(exch, cot):
    row = lax.broadcasted_iota(jnp.int32, exch.shape, 0)
    col = lax.broadcasted_iota(jnp.int32, exch.shape, 1)
    on_diagonal = jnp.where(row == col, exch, 0.0)
    coul = jnp.sum(jnp.sum(on_diagonal, axis=0, keepdims=True), axis=1, keepdims=True)
    return (cot * (jnp.where(row == col, coul, 0.0) - exch)).astype(BF16)


def row_groups(rows, width):
    fits = [n for n in range(1, rows + 1) if rows % n == 0 and rows // n % SUBLANES == 0]
    padded = {n: -(-n * width // LANES) * LANES / n for n in fits}
    least = min(padded.values())
    return min(n for n in fits if padded[n] <= 1.03 * least)


def partials_kernel(blocks, groups, cot_ref, green_ref, chol_ref, trial_ref, hamil_ref, *refs):
    outs, own_ref, part_ref, packed_ref = refs[: blocks - 1], *refs[blocks - 1 :]
    rank = lax.axis_index("chol")
    cot = cot_ref[lax.axis_index("walk")]
    green = green_ref[0]
    nocc, norb = green.shape
    width = norb // blocks
    height = nocc // groups
    total = cot * nn(trial_ref[...].T, hamil_ref[...])
    for v in range(chol_ref.shape[0]):
        vector = chol_ref[v]
        total += nn(kernel_of(nt(vector, green), cot), vector)
    part_ref[...] = total
    for q in range(blocks):
        for r in range(groups):
            packed_ref[q, :, r * width : (r + 1) * width] = part_ref[
                r * height : (r + 1) * height, q * width : (q + 1) * width
            ]
    for k in range(1, blocks):
        outs[k - 1][...] = packed_ref[rank ^ k].astype(BF16)
    own_ref[...] = packed_ref[rank]


def partials(blocks, groups, green, chol, trial, hamil, cot):
    _, nocc, norb = green.shape
    block = (nocc // groups, groups * (norb // blocks))
    vmem = pl.BlockSpec(memory_space=pltpu.VMEM)
    return pl.pallas_call(
        functools.partial(partials_kernel, blocks, groups),
        out_shape=[jax.ShapeDtypeStruct(block, BF16)] * (blocks - 1)
        + [jax.ShapeDtypeStruct(block, F32)],
        in_specs=[pl.BlockSpec(memory_space=pltpu.SMEM)] + [vmem] * 4,
        out_specs=[vmem] * blocks,
        scratch_shapes=[
            pltpu.VMEM((nocc, norb), F32),
            pltpu.VMEM((blocks,) + block, F32),
        ],
        cost_estimate=pl.CostEstimate(
            flops=2 * nocc * norb * (2 * chol.shape[0] * nocc + trial.shape[0]),
            bytes_accessed=2 * (green.size + chol.size + trial.size + hamil.size + 5 * nocc * norb // 4),
            transcendentals=0,
        ),
        compiler_params=pltpu.CompilerParams(vmem_limit_bytes=16 * MIB),
        name="partials",
    )(cot, green, chol, trial, hamil)


def walkers_kernel(order, last, ways, cot_ref, chol_ref, hamil_ref, *refs):
    count = len(order)
    greens, refs = refs[:count], refs[count:]
    if last:
        old_chol, old_bar, d_chol_ref, d_trial_ref, share = refs
    else:
        d_chol_ref, bar_ref, share = refs
    rank = lax.axis_index("walk")
    width = share.shape[2]
    for place in range(ways):

        @pl.when(rank == place)
        def _():
            for n in range(count):
                share[n] = greens[n][0, :, place * width : (place + 1) * width]

    bar = old_bar[...] if last else 0.0
    for n in range(count):
        bar += cot_ref[rank ^ order[n]] * greens[n][0].astype(F32)
    if last:
        d_trial_ref[...] = nt(hamil_ref[...], bar.astype(BF16))
    else:
        bar_ref[...] = bar
    for v in range(chol_ref.shape[0]):
        total = old_chol[v] if last else 0.0
        for n in range(count):
            flipped = nt(greens[n][0], chol_ref[v])
            total += nn(kernel_of(flipped, cot_ref[rank ^ order[n]]), share[n])
        d_chol_ref[v] = total


def walkers(order, last, ways, cot, chol, hamil, greens, old=()):
    vectors, nocc, norb = chol.shape
    width = norb // ways
    vmem = pl.BlockSpec(memory_space=pltpu.VMEM)
    second = (hamil.shape[0], nocc) if last else (nocc, norb)
    return pl.pallas_call(
        functools.partial(walkers_kernel, order, last, ways),
        out_shape=[
            jax.ShapeDtypeStruct((vectors, nocc, width), F32),
            jax.ShapeDtypeStruct(second, F32),
        ],
        in_specs=[pl.BlockSpec(memory_space=pltpu.SMEM)] + [vmem] * (2 + len(greens) + len(old)),
        out_specs=[vmem] * 2,
        scratch_shapes=[pltpu.VMEM((len(order), nocc, width), BF16)],
        cost_estimate=pl.CostEstimate(
            flops=2 * nocc * nocc * vectors * len(order) * (norb + width)
            + (2 * hamil.size * nocc if last else 0),
            bytes_accessed=2 * (chol.size + hamil.size + len(order) * nocc * norb),
            transcendentals=0,
        ),
        compiler_params=pltpu.CompilerParams(vmem_limit_bytes=16 * MIB),
        name="walkers_last" if last else "walkers_first",
    )(cot, chol, hamil, *greens, *old)


def joined_kernel(groups, own_ref, *refs):
    received, out_ref, sum_ref = refs[:-2], refs[-2], refs[-1]
    total = own_ref[...]
    for part in received:
        total += part[...].astype(F32)
    sum_ref[...] = total
    height = total.shape[0]
    width = total.shape[1] // groups
    for r in range(groups):
        out_ref[0, r * height : (r + 1) * height, :] = sum_ref[:, r * width : (r + 1) * width]


def joined(groups, own, received):
    height, long = own.shape
    vmem = pl.BlockSpec(memory_space=pltpu.VMEM)
    return pl.pallas_call(
        functools.partial(joined_kernel, groups),
        out_shape=jax.ShapeDtypeStruct((1, groups * height, long // groups), F32),
        in_specs=[vmem] * (1 + len(received)),
        out_specs=vmem,
        scratch_shapes=[pltpu.VMEM((height, long), F32)],
        cost_estimate=pl.CostEstimate(
            flops=own.size * 4, bytes_accessed=own.size * 16, transcendentals=0
        ),
        compiler_params=pltpu.CompilerParams(vmem_limit_bytes=16 * MIB),
        name="joined",
    )(own, *received)


def swapped(x, axis, bits):
    return lax.ppermute(x, axis, [(i, i ^ bits) for i in range(lax.axis_size(axis))])


def shards(green, chol, trial, hamil, energy_cot):
    ways = lax.axis_size("walk")
    blocks = lax.axis_size("chol")
    _, nocc, norb = green.shape
    groups = row_groups(nocc, norb // blocks)
    far = swapped(green, "walk", 2)
    near = swapped(green, "walk", 1)
    *away, own = partials(blocks, groups, green, chol, trial, hamil, energy_cot)
    received = [swapped(block, "chol", k + 1) for k, block in enumerate(away)]
    first = walkers((0, 1), False, ways, energy_cot, chol, hamil, [green, near])
    other = swapped(far, "walk", 1)
    d_chol, d_trial = walkers((2, 3), True, ways, energy_cot, chol, hamil, [far, other], first)
    d_green = joined(groups, own, received)
    return (d_green, d_chol, d_trial)


def solution(mesh):
    fits = mesh.shape["walk"] == 4 and mesh.shape["chol"] in (2, 4)

    def body(green, *rest):
        if fits and green.shape[0] == 1 and green.shape[1] % SUBLANES == 0:
            return shards(green, *rest)
        return plain(green, *rest)

    return jax.shard_map(
        body,
        mesh=mesh,
        in_specs=(
            P(("groups", "walk"), None, None),
            P(("groups", "chol"), None, None),
            P(("groups", "chol"), None),
            P("chol", None),
            P("groups"),
        ),
        out_specs=(
            P(("groups", "walk"), None, "chol"),
            P(("groups", "chol"), None, "walk"),
            P(("groups", "chol"), None),
        ),
        check_vma=False,
    )
```

time: 101 us -> 52.6 us (0.52)
  waiting for transfers between devices: 55.6 us -> 27.6 us
  matrix products: 20 us -> 0 us
  between operations: 14.1 us -> 0.69 us
  Pallas kernels: 0 us -> 10.6 us
  starting transfers between devices: 0.08 us -> 7.54 us
  local copies, waits for them, and re-layouts: 11.2 us -> 5.34 us
    all_gather x1 -> x0, waiting for transfers between devices: 28.8 us -> none  [shards(): greens = lax.all_gather(green, 'walk', axis=0, tiled=True)]
    ppermute x0 -> x6, waiting for transfers between devices: none -> 27.6 us  [swapped(): lax.ppermute(x, axis, [(i, i ^ bits) for i in range(lax.axis_size(axis))])]
    unnamed x3 -> x0, waiting for transfers between devices: 26.7 us -> none
    dot_general x7 -> x0, matrix products: 20 us -> none  [the longest x1 6.17 us: shards(): jnp.einsum('w,wip->ip', energy_cot, greens, precision=lax.Precision.HIGHE...]
    pallas_call x0 -> x4, Pallas kernels: none -> 10.6 us  [the longest x2 7.04 us: walkers(): pl.pallas_call(functools.partial(walkers_kernel, order, last, ways), out_...]
    ppermute x0 -> x6, starting transfers between devices: none -> 7.54 us  [swapped(): lax.ppermute(x, axis, [(i, i ^ bits) for i in range(lax.axis_size(axis))])]
    unnamed x19 -> x18, local copies, waits for them, and re-layouts: 9.96 us -> 5.34 us
    dynamic_slice x1 -> x0, local copies, waits for them, and re-layouts: 1.24 us -> none  [shards(): lax.dynamic_slice_in_dim(energy_cot, walk_rank * walk_rows, walk_rows, 0)]
  transfers between devices with their start and end apart: 2 -> 6, of which waited for: 2 -> 3; matrix products, arithmetic and copies ran while one was open for 12% -> 0% of each run, Pallas kernels for 0% -> 12%
where the time goes in v1:
time: 52.6 us; the launch traced here: 51.8 us
  waiting for transfers between devices  27.6 us (52%)
  Pallas kernels  10.6 us (20%)
  starting transfers between devices  7.54 us (14%)
  local copies, waits for them, and re-layouts  5.34 us (10%)
  between operations  0.69 us (1%)
    ppermute x6, waiting for transfers between devices, swapped(): lax.ppermute(x, axis, [(i, i ^ bits) for i in range(lax.axis_size(axis))])  27.6 us
    ppermute x6, starting transfers between devices, swapped(): lax.ppermute(x, axis, [(i, i ^ bits) for i in range(lax.axis_size(axis))])  7.54 us
    pallas_call x2, Pallas kernels, walkers(): pl.pallas_call(functools.partial(walkers_kernel, order, last, ways), out_...  7.04 us
    unnamed x18, local copies, waits for them, and re-layouts  5.34 us
    pallas_call x1, Pallas kernels, partials(): pl.pallas_call(functools.partial(partials_kernel, blocks, groups), out_sh...  2.68 us
  transfers between devices with their start and end apart: 6, of which 3 were waited for; matrix products, arithmetic and copies ran while one was open for 0% of the time, Pallas kernels for 12%

profile of v1, /device:TPU:0, one launch (start us, length us, event | category | flops | bytes accessed | tf_op | source)
XLA Modules:
  0.0 51.8 jit_solution(12804953413020770364)
XLA Ops:
  0.6 3.0 %collective-permute-start.3 = (bf16[1,200,1600]{2,1,0:T(8,128)(2,1)}, bf16[1,200,1600]{2,1,0:T(8,128)(2,1)S(1)}, u32[]{:S(2)}, u32[]{:S(2)}) collective-permute-start(bf16[1,200,1600]{2,1,0:T(8,128)(2,1)} %refs_0_.1), channel_id=1, source_target_pairs={{0,2},{1,3},{2,0},{3,1},{4,6},{5,7},{6,4},{7,5},{8,10},{9,11},{10,... | collective-permute-start | bytes 1920008 | tf_op jit(solution)/shard_map/ppermute | solution.py:206
  3.7 0.0 collective-permute-start.5
  3.7 15.2 %collective-permute-done.3.refs_0_ = bf16[1,200,1600]{2,1,0:T(8,128)(2,1)S(1)} collective-permute-done((bf16[1,200,1600]{2,1,0:T(8,128)(2,1)}, bf16[1,200,1600]{2,1,0:T(8,128)(2,1)S(1)}, u32[]{:S(2)}, u32[]{:S(2)}) %collective-permute-start.3) | collective-permute-done | bytes 640032 | tf_op jit(solution)/shard_map/ppermute | solution.py:206
  18.8 0.0 collective-permute-start.4
  18.8 0.0 copy-start
  18.8 1.3 %copy-done = bf16[2,200,1600]{2,1,0:T(8,128)(2,1)S(1)} copy-done((bf16[2,200,1600]{2,1,0:T(8,128)(2,1)S(1)}, bf16[2,200,1600]{2,1,0:T(8,128)(2,1)}, u32[]{:S(2)}) %copy-start) | copy-done | bytes 1280024
  20.2 0.0 copy-start.2
  20.2 1.3 %copy-done.2 = bf16[400,1600]{1,0:T(8,128)(2,1)S(1)} copy-done((bf16[400,1600]{1,0:T(8,128)(2,1)S(1)}, bf16[400,1600]{1,0:T(8,128)(2,1)}, u32[]{:S(2)}) %copy-start.2) | copy-done | bytes 1280024
  21.5 0.0 copy-start.4
  21.5 1.1 %copy-done.4 = bf16[1,200,1600]{2,1,0:T(8,128)(2,1)S(1)} copy-done((bf16[1,200,1600]{2,1,0:T(8,128)(2,1)S(1)}, bf16[1,200,1600]{2,1,0:T(8,128)(2,1)}, u32[]{:S(2)}) %copy-start.4) | copy-done | bytes 640024
  22.6 0.0 copy-start.6
  22.6 0.9 %copy-done.6 = bf16[400,200]{1,0:T(8,128)(2,1)S(1)} copy-done((bf16[400,200]{1,0:T(8,128)(2,1)S(1)}, bf16[400,200]{1,0:T(8,128)(2,1)}, u32[]{:S(2)}) %copy-start.6) | copy-done | bytes 160024
  23.5 0.0 copy-start.7
  23.5 0.7 %copy-done.7 = f32[4]{0:T(128)S(1)} copy-done((f32[4]{0:T(128)S(1)}, f32[4]{0:T(128)}, u32[]{:S(2)}) %copy-start.7) | copy-done | bytes 40
  24.2 0.0 copy-start.1
  24.2 0.0 copy-start.3
  24.2 0.0 copy-start.8
  24.2 2.7 %partials.1 = (bf16[40,2000]{1,0:T(8,128)(2,1)S(1)}, bf16[40,2000]{1,0:T(8,128)(2,1)S(1)}, bf16[40,2000]{1,0:T(8,128)(2,1)S(1)}, f32[40,2000]{1,0:T(8,128)S(1)}) custom-call(f32[4]{0:T(128)S(1)} %copy-done.7, bf16[1,200,1600]{2,1,0:T(8,128)(2,1)S(1)} %copy-done.4, bf16[2,200,1600]{2,1,0:T(8,128)(2,1)S(1)} %copy-done, bf16[400,200]{1,0:T(8,128)(2,1)S(1)} %copy-done.6, ...), custom_call_target="tpu_custom_call" | custom-call | flops 768000000 | bytes 4160000 | tf_op jit(solution)/shard_map/partials/pallas_call | solution.py:100
  26.9 0.0 copy-start.5
  26.9 1.9 %collective-permute-start = (bf16[40,2000]{1,0:T(8,128)(2,1)S(1)}, bf16[40,2000]{1,0:T(8,128)(2,1)S(1)}, u32[]{:S(2)}, u32[]{:S(2)}) collective-permute-start(bf16[40,2000]{1,0:T(8,128)(2,1)S(1)} %get-tuple-element.12), channel_id=1, source_target_pairs={{0,4},{4,0},{8,12},{12,8},{1,5},{5,1},{9,13},{13,9},{2,6},{6,2},{1... | collective-permute-start | bytes 480008 | tf_op jit(solution)/shard_map/ppermute | solution.py:206
  28.8 2.6 %collective-permute-start.1 = (bf16[40,2000]{1,0:T(8,128)(2,1)S(1)}, bf16[40,2000]{1,0:T(8,128)(2,1)S(1)}, u32[]{:S(2)}, u32[]{:S(2)}) collective-permute-start(bf16[40,2000]{1,0:T(8,128)(2,1)S(1)} %get-tuple-element.13), channel_id=1, source_target_pairs={{0,8},{4,12},{8,0},{12,4},{1,9},{5,13},{9,1},{13,5},{2,10},{6,14},... | collective-permute-start | bytes 480008 | tf_op jit(solution)/shard_map/ppermute | solution.py:206
  31.4 0.0 collective-permute-start.2
  31.4 5.3 %collective-permute-done.refs_0_ = bf16[40,2000]{1,0:T(8,128)(2,1)S(1)} collective-permute-done((bf16[40,2000]{1,0:T(8,128)(2,1)S(1)}, bf16[40,2000]{1,0:T(8,128)(2,1)S(1)}, u32[]{:S(2)}, u32[]{:S(2)}) %collective-permute-start) | collective-permute-done | bytes 160032 | tf_op jit(solution)/shard_map/ppermute | solution.py:206
  36.7 7.1 %collective-permute-done.1.refs_1_ = bf16[40,2000]{1,0:T(8,128)(2,1)S(1)} collective-permute-done((bf16[40,2000]{1,0:T(8,128)(2,1)S(1)}, bf16[40,2000]{1,0:T(8,128)(2,1)S(1)}, u32[]{:S(2)}, u32[]{:S(2)}) %collective-permute-start.1) | collective-permute-done | bytes 160032 | tf_op jit(solution)/shard_map/ppermute | solution.py:206
  43.8 0.0 collective-permute-done.2.refs_2_
  43.8 0.9 %joined.1 = f32[1,200,400]{2,1,0:T(8,128)} custom-call(f32[40,2000]{1,0:T(8,128)S(1)} %get-tuple-element.11.own_ref, bf16[40,2000]{1,0:T(8,128)(2,1)S(1)} %collective-permute-done.refs_0_, bf16[40,2000]{1,0:T(8,128)(2,1)S(1)} %collective-permute-done.1.refs_1_, bf16[40,2000]{1,0:T(8,128)(2,1)S(1)} %collective-permute-done.2.refs_2_), custom_call_target="tpu_custom_call" | custom-call | flops 320000 | bytes 1280000 | tf_op jit(solution)/shard_map/joined/pallas_call | solution.py:191
  44.7 0.0 collective-permute-done.5.refs_1_
  44.7 0.0 copy-done.1
  44.7 0.0 copy-done.3
  44.7 0.0 copy-done.8
  44.7 0.0 copy-done.5
  44.7 2.5 %walkers_first.1 = (f32[2,200,400]{2,1,0:T(8,128)S(1)}, f32[200,1600]{1,0:T(8,128)S(1)}) custom-call(f32[4]{0:T(128)S(1)} %copy-done.8, bf16[2,200,1600]{2,1,0:T(8,128)(2,1)S(1)} %copy-done.1, bf16[400,1600]{1,0:T(8,128)(2,1)S(1)} %copy-done.3, bf16[1,200,1600]{2,1,0:T(8,128)(2,1)S(1)} %copy-done.5, bf16[1,200,1600]{2,1,0:T(8,128)(2,1)S(1)} %collective-permute-done.5.refs_1_), custom_call_target="tpu_custom_call" | custom-call | flops 640000000 | bytes 3840000 | tf_op jit(solution)/shard_map/walkers_first/pallas_call | solution.py:156
  47.3 0.0 collective-permute-done.4.refs_1_
  47.3 4.5 %walkers_last.1 = (f32[2,200,400]{2,1,0:T(8,128)}, f32[400,200]{1,0:T(8,128)}) custom-call(f32[4]{0:T(128)S(1)} %copy-done.8, bf16[2,200,1600]{2,1,0:T(8,128)(2,1)S(1)} %copy-done.1, bf16[400,1600]{1,0:T(8,128)(2,1)S(1)} %copy-done.3, bf16[1,200,1600]{2,1,0:T(8,128)(2,1)S(1)} %collective-permute-done.3.refs_0_, ...), custom_call_target="tpu_custom_call" | custom-call | flops 896000000 | bytes 3840000 | tf_op jit(solution)/shard_map/walkers_last/pallas_call | solution.py:156
Async XLA Ops:
  0.6 18.2 %collective-permute-start.3 = (bf16[1,200,1600]{2,1,0:T(8,128)(2,1)}, bf16[1,200,1600]{2,1,0:T(8,128)(2,1)S(1)}, u32[]{:S(2)}, u32[]{:S(2)}) collective-permute-start(bf16[1,200,1600]{2,1,0:T(8,128)(2,1)} %refs_0_.1), channel_id=1, source_target_pairs={{0,2},{1,3},{2,0},{3,1},{4,6},{5,7},{6,4},{7,5},{8,10},{9,11},{10,... | collective-permute-start | bytes 1920008 | tf_op jit(solution)/shard_map/ppermute | solution.py:206
  3.7 41.1 %collective-permute-start.5 = (bf16[1,200,1600]{2,1,0:T(8,128)(2,1)}, bf16[1,200,1600]{2,1,0:T(8,128)(2,1)S(1)}, u32[]{:S(2)}, u32[]{:S(2)}) collective-permute-start(bf16[1,200,1600]{2,1,0:T(8,128)(2,1)} %refs_0_.1), channel_id=1, source_target_pairs={{0,1},{1,0},{2,3},{3,2},{4,5},{5,4},{6,7},{7,6},{8,9},{9,8},{10,11... | collective-permute-start | bytes 1920008 | tf_op jit(solution)/shard_map/ppermute | solution.py:206
  18.8 28.5 %collective-permute-start.4 = (bf16[1,200,1600]{2,1,0:T(8,128)(2,1)S(1)}, bf16[1,200,1600]{2,1,0:T(8,128)(2,1)S(1)}, u32[]{:S(2)}, u32[]{:S(2)}) collective-permute-start(bf16[1,200,1600]{2,1,0:T(8,128)(2,1)S(1)} %collective-permute-done.3.refs_0_), channel_id=1, source_target_pairs={{0,1},{1,0},{2,3},{3,2},{4,5},{5,4},{6,7},{7,6},{8,9},{9,8},{10,11... | collective-permute-start | bytes 1920008 | tf_op jit(solution)/shard_map/ppermute | solution.py:206
  18.8 1.3 %copy-start = (bf16[2,200,1600]{2,1,0:T(8,128)(2,1)S(1)}, bf16[2,200,1600]{2,1,0:T(8,128)(2,1)}, u32[]{:S(2)}) copy-start(bf16[2,200,1600]{2,1,0:T(8,128)(2,1)} %chol_ref.5) | copy-start | bytes 3840004
  20.2 1.3 %copy-start.2 = (bf16[400,1600]{1,0:T(8,128)(2,1)S(1)}, bf16[400,1600]{1,0:T(8,128)(2,1)}, u32[]{:S(2)}) copy-start(bf16[400,1600]{1,0:T(8,128)(2,1)} %hamil_ref.5) | copy-start | bytes 3840004
  21.5 1.1 %copy-start.4 = (bf16[1,200,1600]{2,1,0:T(8,128)(2,1)S(1)}, bf16[1,200,1600]{2,1,0:T(8,128)(2,1)}, u32[]{:S(2)}) copy-start(bf16[1,200,1600]{2,1,0:T(8,128)(2,1)} %refs_0_.1) | copy-start | bytes 1920004
  22.6 0.9 %copy-start.6 = (bf16[400,200]{1,0:T(8,128)(2,1)S(1)}, bf16[400,200]{1,0:T(8,128)(2,1)}, u32[]{:S(2)}) copy-start(bf16[400,200]{1,0:T(8,128)(2,1)} %trial_ref.1) | copy-start | bytes 480004
  23.5 0.7 %copy-start.7 = (f32[4]{0:T(128)S(1)}, f32[4]{0:T(128)}, u32[]{:S(2)}) copy-start(f32[4]{0:T(128)} %cot_ref.5) | copy-start | bytes 52
  24.2 20.6 %copy-start.1 = (bf16[2,200,1600]{2,1,0:T(8,128)(2,1)S(1)}, bf16[2,200,1600]{2,1,0:T(8,128)(2,1)}, u32[]{:S(2)}) copy-start(bf16[2,200,1600]{2,1,0:T(8,128)(2,1)} %chol_ref.5) | copy-start | bytes 3840004
  24.2 20.6 %copy-start.3 = (bf16[400,1600]{1,0:T(8,128)(2,1)S(1)}, bf16[400,1600]{1,0:T(8,128)(2,1)}, u32[]{:S(2)}) copy-start(bf16[400,1600]{1,0:T(8,128)(2,1)} %hamil_ref.5) | copy-start | bytes 3840004
  24.2 20.6 %copy-start.8 = (f32[4]{0:T(128)S(1)}, f32[4]{0:T(128)}, u32[]{:S(2)}) copy-start(f32[4]{0:T(128)} %cot_ref.5) | copy-start | bytes 52
  26.9 17.9 %copy-start.5 = (bf16[1,200,1600]{2,1,0:T(8,128)(2,1)S(1)}, bf16[1,200,1600]{2,1,0:T(8,128)(2,1)}, u32[]{:S(2)}) copy-start(bf16[1,200,1600]{2,1,0:T(8,128)(2,1)} %refs_0_.1) | copy-start | bytes 1920004
  26.9 9.8 %collective-permute-start = (bf16[40,2000]{1,0:T(8,128)(2,1)S(1)}, bf16[40,2000]{1,0:T(8,128)(2,1)S(1)}, u32[]{:S(2)}, u32[]{:S(2)}) collective-permute-start(bf16[40,2000]{1,0:T(8,128)(2,1)S(1)} %get-tuple-element.12), channel_id=1, source_target_pairs={{0,4},{4,0},{8,12},{12,8},{1,5},{5,1},{9,13},{13,9},{2,6},{6,2},{1... | collective-permute-start | bytes 480008 | tf_op jit(solution)/shard_map/ppermute | solution.py:206
  28.8 15.0 %collective-permute-start.1 = (bf16[40,2000]{1,0:T(8,128)(2,1)S(1)}, bf16[40,2000]{1,0:T(8,128)(2,1)S(1)}, u32[]{:S(2)}, u32[]{:S(2)}) collective-permute-start(bf16[40,2000]{1,0:T(8,128)(2,1)S(1)} %get-tuple-element.13), channel_id=1, source_target_pairs={{0,8},{4,12},{8,0},{12,4},{1,9},{5,13},{9,1},{13,5},{2,10},{6,14},... | collective-permute-start | bytes 480008 | tf_op jit(solution)/shard_map/ppermute | solution.py:206
  31.4 12.4 %collective-permute-start.2 = (bf16[40,2000]{1,0:T(8,128)(2,1)S(1)}, bf16[40,2000]{1,0:T(8,128)(2,1)S(1)}, u32[]{:S(2)}, u32[]{:S(2)}) collective-permute-start(bf16[40,2000]{1,0:T(8,128)(2,1)S(1)} %get-tuple-element.14), channel_id=1, source_target_pairs={{0,12},{4,8},{8,4},{12,0},{1,13},{5,9},{9,5},{13,1},{2,14},{6,10},... | collective-permute-start | bytes 480008 | tf_op jit(solution)/shard_map/ppermute | solution.py:206

commit v2 on v1

--- a/solution.py
+++ b/solution.py
@@ -70,60 +70,138 @@
     return min(n for n in fits if padded[n] <= 1.03 * least)
 
 
-def partials_kernel(blocks, groups, cot_ref, green_ref, chol_ref, trial_ref, hamil_ref, *refs):
-    outs, own_ref, part_ref, packed_ref = refs[: blocks - 1], *refs[blocks - 1 :]
+def half_of(half, kernels, cot, chol_ref, trial, hamil_ref, part_ref, packed_ref, groups):
+    nocc, norb = chol_ref.shape[1:]
+    width = norb // 4
+    height = nocc // groups
+    begin = half * 2 * width
+    window = slice(begin // LANES * LANES, begin + 2 * width)
+    total = cot * nn(trial, hamil_ref[:, window])
+    for v, kernel in enumerate(kernels):
+        total += nn(kernel, chol_ref[v, :, window])
+    part_ref[:, : total.shape[1]] = total
+    for q in range(2):
+        left = begin - window.start + q * width
+        for r in range(groups):
+            packed_ref[q, :, r * width : (r + 1) * width] = part_ref[
+                r * height : (r + 1) * height, left : left + width
+            ]
+
+
+def crossing_kernel(groups, *refs):
+    cot_in, green_in, chol_in, trial_in, hamil_in = refs[:5]
+    second_ref, third_ref, kernel_ref, green_ref, chol_ref, trial_ref, hamil_ref = refs[5:12]
+    cot_ref, part_ref, packed_ref, sems = refs[12:]
+    vectors = chol_ref.shape[0]
+    copies = [pltpu.make_async_copy(green_in, green_ref, sems.at[0])]
+    for v in range(vectors):
+        copies.append(pltpu.make_async_copy(chol_in.at[v], chol_ref.at[v], sems.at[1 + v]))
+    copies.append(pltpu.make_async_copy(trial_in, trial_ref, sems.at[1 + vectors]))
+    copies.append(pltpu.make_async_copy(hamil_in, hamil_ref, sems.at[2 + vectors]))
+    copies.append(pltpu.make_async_copy(cot_in, cot_ref, sems.at[3 + vectors]))
+    for copy in copies[-1:] + copies[:-1]:
+        copy.start()
+    rank = lax.axis_index("chol")
+    copies[-1].wait()
+    cot = cot_ref[lax.axis_index("walk")]
+    copies[0].wait()
+    for v in range(vectors):
+        copies[1 + v].wait()
+        kernel_ref[v] = kernel_of(nt(chol_ref[v], green_ref[0]), cot)
+    copies[1 + vectors].wait()
+    copies[2 + vectors].wait()
+    for half in range(2):
+
+        @pl.when(rank // 2 != half)
+        def _():
+            kernels = [kernel_ref[v] for v in range(vectors)]
+            trial = trial_ref[...].T
+            half_of(half, kernels, cot, chol_ref, trial, hamil_ref, part_ref, packed_ref, groups)
+
+    second_ref[...] = packed_ref[rank % 2].astype(BF16)
+    third_ref[...] = packed_ref[1 - rank % 2].astype(BF16)
+
+
+def staying_kernel(groups, *refs):
+    cot_ref, kernel_ref, chol_ref, trial_ref, hamil_ref = refs[:5]
+    first_ref, own_ref, part_ref, packed_ref = refs[5:]
     rank = lax.axis_index("chol")
     cot = cot_ref[lax.axis_index("walk")]
-    green = green_ref[0]
-    nocc, norb = green.shape
-    width = norb // blocks
-    height = nocc // groups
-    total = cot * nn(trial_ref[...].T, hamil_ref[...])
-    for v in range(chol_ref.shape[0]):
-        vector = chol_ref[v]
-        total += nn(kernel_of(nt(vector, green), cot), vector)
-    part_ref[...] = total
-    for q in range(blocks):
-        for r in range(groups):
-            packed_ref[q, :, r * width : (r + 1) * width] = part_ref[
-                r * height : (r + 1) * height, q * width : (q + 1) * width
-            ]
-    for k in range(1, blocks):
-        outs[k - 1][...] = packed_ref[rank ^ k].astype(BF16)
-    own_ref[...] = packed_ref[rank]
-
-
-def partials(blocks, groups, green, chol, trial, hamil, cot):
+    for half in range(2):
+
+        @pl.when(rank // 2 == half)
+        def _():
+            kernels = [kernel_ref[v] for v in range(chol_ref.shape[0])]
+            trial = trial_ref[...].T
+            half_of(half, kernels, cot, chol_ref, trial, hamil_ref, part_ref, packed_ref, groups)
+
+    first_ref[...] = packed_ref[1 - rank % 2].astype(BF16)
+    own_ref[...] = packed_ref[rank % 2]
+
+
+def half_scratch(nocc, norb, block):
+    wide = -(-(norb // 2) // LANES) * LANES + LANES
+    return [pltpu.VMEM((nocc, wide), F32), pltpu.VMEM((2,) + block, F32)]
+
+
+def shape_of(x):
+    return jax.ShapeDtypeStruct(x.shape, x.dtype)
+
+
+def crossing(groups, cot, green, chol, trial, hamil):
     _, nocc, norb = green.shape
-    block = (nocc // groups, groups * (norb // blocks))
+    vectors = chol.shape[0]
+    block = (nocc // groups, groups * (norb // 4))
+    vmem = pl.BlockSpec(memory_space=pltpu.VMEM)
+    loaded = (cot, green, chol, trial, hamil)
+    loaded = [pltpu.with_memory_space_constraint(x, pltpu.HBM) for x in loaded]
+    return pl.pallas_call(
+        functools.partial(crossing_kernel, groups),
+        out_shape=[jax.ShapeDtypeStruct(block, BF16)] * 2
+        + [jax.ShapeDtypeStruct((vectors, nocc, nocc), BF16)]
+        + [shape_of(x) for x in (green, chol, trial, hamil)],
+        in_specs=[pl.BlockSpec(memory_space=pltpu.HBM)] * 5,
+        out_specs=[vmem] * 7,
+        scratch_shapes=[pltpu.SMEM(cot.shape, F32)]
+        + half_scratch(nocc, norb, block)
+        + [pltpu.SemaphoreType.DMA((4 + vectors,))],
+        cost_estimate=pl.CostEstimate(
+            flops=nocc * norb * (3 * vectors * nocc + trial.shape[0]),
+            bytes_accessed=2 * (green.size + chol.size + trial.size + hamil.size),
+            transcendentals=0,
+        ),
+        compiler_params=pltpu.CompilerParams(vmem_limit_bytes=16 * MIB),
+        name="crossing",
+    )(*loaded)
+
+
+def staying(groups, cot, kernels, chol, trial, hamil):
+    vectors, nocc, norb = chol.shape
+    block = (nocc // groups, groups * (norb // 4))
     vmem = pl.BlockSpec(memory_space=pltpu.VMEM)
     return pl.pallas_call(
-        functools.partial(partials_kernel, blocks, groups),
-        out_shape=[jax.ShapeDtypeStruct(block, BF16)] * (blocks - 1)
-        + [jax.ShapeDtypeStruct(block, F32)],
+        functools.partial(staying_kernel, groups),
+        out_shape=[jax.ShapeDtypeStruct(block, BF16), jax.ShapeDtypeStruct(block, F32)],
         in_specs=[pl.BlockSpec(memory_space=pltpu.SMEM)] + [vmem] * 4,
-        out_specs=[vmem] * blocks,
-        scratch_shapes=[
-            pltpu.VMEM((nocc, norb), F32),
-            pltpu.VMEM((blocks,) + block, F32),
-        ],
+        out_specs=[vmem] * 2,
+        scratch_shapes=half_scratch(nocc, norb, block),
         cost_estimate=pl.CostEstimate(
-            flops=2 * nocc * norb * (2 * chol.shape[0] * nocc + trial.shape[0]),
-            bytes_accessed=2 * (green.size + chol.size + trial.size + hamil.size + 5 * nocc * norb // 4),
+            flops=nocc * norb * (vectors * nocc + trial.shape[0]),
+            bytes_accessed=2 * (chol.size + trial.size + hamil.size),
             transcendentals=0,
         ),
         compiler_params=pltpu.CompilerParams(vmem_limit_bytes=16 * MIB),
-        name="partials",
-    )(cot, green, chol, trial, hamil)
-
-
-def walkers_kernel(order, last, ways, cot_ref, chol_ref, hamil_ref, *refs):
+        name="staying",
+    )(cot, kernels, chol, trial, hamil)
+
+
+def walkers_kernel(order, old, last, ways, cot_ref, chol_ref, *refs):
     count = len(order)
     greens, refs = refs[:count], refs[count:]
-    if last:
-        old_chol, old_bar, d_chol_ref, d_trial_ref, share = refs
-    else:
-        d_chol_ref, bar_ref, share = refs
+    old_chol, old_bar = refs[:2] if old else (None, None)
+    refs = refs[2 * old :]
+    hamil_ref, refs = (refs[0], refs[1:]) if last else (None, refs)
+    d_chol_ref, second_ref, share = refs
     rank = lax.axis_index("walk")
     width = share.shape[2]
     for place in range(ways):
@@ -133,44 +211,45 @@
             for n in range(count):
                 share[n] = greens[n][0, :, place * width : (place + 1) * width]
 
-    bar = old_bar[...] if last else 0.0
-    for n in range(count):
-        bar += cot_ref[rank ^ order[n]] * greens[n][0].astype(F32)
-    if last:
-        d_trial_ref[...] = nt(hamil_ref[...], bar.astype(BF16))
-    else:
-        bar_ref[...] = bar
     for v in range(chol_ref.shape[0]):
-        total = old_chol[v] if last else 0.0
+        total = old_chol[v] if old else 0.0
         for n in range(count):
             flipped = nt(greens[n][0], chol_ref[v])
             total += nn(kernel_of(flipped, cot_ref[rank ^ order[n]]), share[n])
         d_chol_ref[v] = total
-
-
-def walkers(order, last, ways, cot, chol, hamil, greens, old=()):
+    bar = old_bar[...] if old else 0.0
+    for n in range(count):
+        bar += cot_ref[rank ^ order[n]] * greens[n][0].astype(F32)
+    if last:
+        second_ref[...] = nt(hamil_ref[...], bar.astype(BF16))
+    else:
+        second_ref[...] = bar
+
+
+def walkers(order, ways, cot, chol, greens, old=(), hamil=None):
     vectors, nocc, norb = chol.shape
     width = norb // ways
+    last = hamil is not None
+    rest = (*greens, *old) + ((hamil,) if last else ())
     vmem = pl.BlockSpec(memory_space=pltpu.VMEM)
     second = (hamil.shape[0], nocc) if last else (nocc, norb)
     return pl.pallas_call(
-        functools.partial(walkers_kernel, order, last, ways),
+        functools.partial(walkers_kernel, order, bool(old), last, ways),
         out_shape=[
             jax.ShapeDtypeStruct((vectors, nocc, width), F32),
             jax.ShapeDtypeStruct(second, F32),
         ],
-        in_specs=[pl.BlockSpec(memory_space=pltpu.SMEM)] + [vmem] * (2 + len(greens) + len(old)),
+        in_specs=[pl.BlockSpec(memory_space=pltpu.SMEM)] + [vmem] * (1 + len(rest)),
         out_specs=[vmem] * 2,
         scratch_shapes=[pltpu.VMEM((len(order), nocc, width), BF16)],
         cost_estimate=pl.CostEstimate(
             flops=2 * nocc * nocc * vectors * len(order) * (norb + width)
             + (2 * hamil.size * nocc if last else 0),
-            bytes_accessed=2 * (chol.size + hamil.size + len(order) * nocc * norb),
+            bytes_accessed=2 * (chol.size + len(order) * nocc * norb),
             transcendentals=0,
         ),
         compiler_params=pltpu.CompilerParams(vmem_limit_bytes=16 * MIB),
-        name="walkers_last" if last else "walkers_first",
-    )(cot, chol, hamil, *greens, *old)
+    )(cot, chol, *rest)
 
 
 def joined_kernel(groups, own_ref, *refs):
@@ -208,22 +287,27 @@
 
 def shards(green, chol, trial, hamil, energy_cot):
     ways = lax.axis_size("walk")
-    blocks = lax.axis_size("chol")
     _, nocc, norb = green.shape
-    groups = row_groups(nocc, norb // blocks)
+    groups = row_groups(nocc, norb // lax.axis_size("chol"))
     far = swapped(green, "walk", 2)
     near = swapped(green, "walk", 1)
-    *away, own = partials(blocks, groups, green, chol, trial, hamil, energy_cot)
-    received = [swapped(block, "chol", k + 1) for k, block in enumerate(away)]
-    first = walkers((0, 1), False, ways, energy_cot, chol, hamil, [green, near])
+    second, third, kernels, green, chol, trial, hamil = crossing(
+        groups, energy_cot, green, chol, trial, hamil
+    )
+    from_second = swapped(second, "chol", 2)
+    from_third = swapped(third, "chol", 3)
+    first, own = staying(groups, energy_cot, kernels, chol, trial, hamil)
+    from_first = swapped(first, "chol", 1)
+    sums = walkers((0, 1), ways, energy_cot, chol, [green, near])
     other = swapped(far, "walk", 1)
-    d_chol, d_trial = walkers((2, 3), True, ways, energy_cot, chol, hamil, [far, other], first)
-    d_green = joined(groups, own, received)
+    sums = walkers((2,), ways, energy_cot, chol, [far], sums)
+    d_chol, d_trial = walkers((3,), ways, energy_cot, chol, [other], sums, hamil)
+    d_green = joined(groups, own, [from_first, from_second, from_third])
     return (d_green, d_chol, d_trial)
 
 
 def solution(mesh):
-    fits = mesh.shape["walk"] == 4 and mesh.shape["chol"] in (2, 4)
+    fits = mesh.shape["walk"] == 4 and mesh.shape["chol"] == 4
 
     def body(green, *rest):
         if fits and green.shape[0] == 1 and green.shape[1] % SUBLANES == 0:

time: 52.6 us -> 50.8 us (0.966)
  local copies, waits for them, and re-layouts: 5.34 us -> 0.01 us
  Pallas kernels: 10.6 us -> 14.2 us
    unnamed x18 -> x2, local copies, waits for them, and re-layouts: 5.34 us -> 0.01 us
    pallas_call x3 -> x5, Pallas kernels: 9.72 us -> 13.3 us  [the longest x3 8.37 us: walkers(): pl.pallas_call(functools.partial(walkers_kernel, order, bool(old), last,...]
  transfers between devices with their start and end apart: 6 -> 6, of which waited for: 3 -> 3; matrix products, arithmetic and copies ran while one was open for 0% -> 0% of each run, Pallas kernels for 12% -> 22%
where the time goes in v2:
time: 50.8 us; the launch traced here: 50 us
  waiting for transfers between devices  27.6 us (54%)
  Pallas kernels  14.2 us (28%)
  starting transfers between devices  7.5 us (15%)
  between operations  0.69 us (1%)
    ppermute x6, waiting for transfers between devices, swapped(): lax.ppermute(x, axis, [(i, i ^ bits) for i in range(lax.axis_size(axis))])  27.6 us
    pallas_call x3, Pallas kernels, walkers(): pl.pallas_call(functools.partial(walkers_kernel, order, bool(old), last,...  8.37 us
    ppermute x6, starting transfers between devices, swapped(): lax.ppermute(x, axis, [(i, i ^ bits) for i in range(lax.axis_size(axis))])  7.5 us
    pallas_call x1, Pallas kernels, crossing(): pl.pallas_call(functools.partial(crossing_kernel, groups), out_shape=[jax...  3.5 us
    pallas_call x1, Pallas kernels, staying(): pl.pallas_call(functools.partial(staying_kernel, groups), out_shape=[jax....  1.39 us
  transfers between devices with their start and end apart: 6, of which 3 were waited for; matrix products, arithmetic and copies ran while one was open for 0% of the time, Pallas kernels for 22%

profile of v2, /device:TPU:0, one launch (start us, length us, event | category | flops | bytes accessed | tf_op | source)
XLA Modules:
  0.0 50.0 jit_solution(1010992881778500647)
XLA Ops:
  0.6 0.0 copy-start
  0.6 3.0 %collective-permute-start.3 = (bf16[1,200,1600]{2,1,0:T(8,128)(2,1)}, bf16[1,200,1600]{2,1,0:T(8,128)(2,1)S(1)}, u32[]{:S(2)}, u32[]{:S(2)}) collective-permute-start(bf16[1,200,1600]{2,1,0:T(8,128)(2,1)} %refs_1_.1), channel_id=1, source_target_pairs={{0,2},{1,3},{2,0},{3,1},{4,6},{5,7},{6,4},{7,5},{8,10},{9,11},{10,... | collective-permute-start | bytes 1920008 | tf_op jit(solution)/shard_map/ppermute | solution.py:285
  3.7 0.0 collective-permute-start.5
  3.7 15.2 %collective-permute-done.3.refs_0_ = bf16[1,200,1600]{2,1,0:T(8,128)(2,1)S(1)} collective-permute-done((bf16[1,200,1600]{2,1,0:T(8,128)(2,1)}, bf16[1,200,1600]{2,1,0:T(8,128)(2,1)S(1)}, u32[]{:S(2)}, u32[]{:S(2)}) %collective-permute-start.3) | collective-permute-done | bytes 640032 | tf_op jit(solution)/shard_map/ppermute | solution.py:285
  18.8 0.0 collective-permute-start.4
  18.8 3.5 %crossing.1 = (bf16[40,2000]{1,0:T(8,128)(2,1)S(1)}, bf16[40,2000]{1,0:T(8,128)(2,1)S(1)}, bf16[2,200,200]{2,1,0:T(8,128)(2,1)S(1)}, bf16[1,200,1600]{2,1,0:T(8,...) custom-call(f32[4]{0:T(128)} %cot_ref.5, ...), custom_call_target="tpu_custom_call" | custom-call | flops 512000000 | bytes 3360000 | tf_op jit(solution)/shard_map/crossing/pallas_call | solution.py:158
  22.4 0.0 copy-done
  22.4 1.4 %staying.1 = (bf16[40,2000]{1,0:T(8,128)(2,1)S(1)}, f32[40,2000]{1,0:T(8,128)S(1)}) custom-call(f32[4]{0:T(128)S(1)} %copy-done, bf16[2,200,200]{2,1,0:T(8,128)(2,1)S(1)} %get-tuple-element.18.refs_1_, bf16[2,200,1600]{2,1,0:T(8,128)(2,1)S(1)} %get-tuple-element.19.refs_2_.chol_ref, bf16[400,200]{1,0:T(8,128)(2,1)S(1)} %get-tuple-element.20.refs_3_, ...), custom_call_target="tpu_custom_call" | custom-call | flops 256000000 | bytes 2720000 | tf_op jit(solution)/shard_map/staying/pallas_call | solution.py:182
  23.8 1.9 %collective-permute-start = (bf16[40,2000]{1,0:T(8,128)(2,1)S(1)}, bf16[40,2000]{1,0:T(8,128)(2,1)S(1)}, u32[]{:S(2)}, u32[]{:S(2)}) collective-permute-start(bf16[40,2000]{1,0:T(8,128)(2,1)S(1)} %get-tuple-element.23), channel_id=1, source_target_pairs={{0,4},{4,0},{8,12},{12,8},{1,5},{5,1},{9,13},{13,9},{2,6},{6,2},{1... | collective-permute-start | bytes 480008 | tf_op jit(solution)/shard_map/ppermute | solution.py:285
  25.6 2.6 %collective-permute-start.1 = (bf16[40,2000]{1,0:T(8,128)(2,1)S(1)}, bf16[40,2000]{1,0:T(8,128)(2,1)S(1)}, u32[]{:S(2)}, u32[]{:S(2)}) collective-permute-start(bf16[40,2000]{1,0:T(8,128)(2,1)S(1)} %get-tuple-element.24), channel_id=1, source_target_pairs={{0,8},{4,12},{8,0},{12,4},{1,9},{5,13},{9,1},{13,5},{2,10},{6,14},... | collective-permute-start | bytes 480008 | tf_op jit(solution)/shard_map/ppermute | solution.py:285
  28.2 0.0 collective-permute-start.2
  28.2 5.4 %collective-permute-done.refs_0_ = bf16[40,2000]{1,0:T(8,128)(2,1)S(1)} collective-permute-done((bf16[40,2000]{1,0:T(8,128)(2,1)S(1)}, bf16[40,2000]{1,0:T(8,128)(2,1)S(1)}, u32[]{:S(2)}, u32[]{:S(2)}) %collective-permute-start) | collective-permute-done | bytes 160032 | tf_op jit(solution)/shard_map/ppermute | solution.py:285
  33.6 7.1 %collective-permute-done.1.refs_1_ = bf16[40,2000]{1,0:T(8,128)(2,1)S(1)} collective-permute-done((bf16[40,2000]{1,0:T(8,128)(2,1)S(1)}, bf16[40,2000]{1,0:T(8,128)(2,1)S(1)}, u32[]{:S(2)}, u32[]{:S(2)}) %collective-permute-start.1) | collective-permute-done | bytes 160032 | tf_op jit(solution)/shard_map/ppermute | solution.py:285
  40.7 0.0 collective-permute-done.2.refs_2_
  40.7 0.9 %joined.1 = f32[1,200,400]{2,1,0:T(8,128)} custom-call(f32[40,2000]{1,0:T(8,128)S(1)} %get-tuple-element.22.own_ref, bf16[40,2000]{1,0:T(8,128)(2,1)S(1)} %collective-permute-done.refs_0_, bf16[40,2000]{1,0:T(8,128)(2,1)S(1)} %collective-permute-done.1.refs_1_, bf16[40,2000]{1,0:T(8,128)(2,1)S(1)} %collective-permute-done.2.refs_2_), custom_call_target="tpu_custom_call" | custom-call | flops 320000 | bytes 1280000 | tf_op jit(solution)/shard_map/joined/pallas_call | solution.py:270
  41.6 0.0 collective-permute-done.5.refs_1_
  41.6 2.5 %shard_map.76 = (f32[2,200,400]{2,1,0:T(8,128)S(1)}, f32[200,1600]{1,0:T(8,128)S(1)}) custom-call(f32[4]{0:T(128)S(1)} %copy-done, bf16[2,200,1600]{2,1,0:T(8,128)(2,1)S(1)} %get-tuple-element.19.refs_2_.chol_ref, bf16[1,200,1600]{2,1,0:T(8,128)(2,1)S(1)} %get-tuple-element.26.refs_0_, bf16[1,200,1600]{2,1,0:T(8,128)(2,1)S(1)} %collective-permute-done.5.refs_1_), custom_call_target="tpu_custom_call" | custom-call | flops 640000000 | bytes 2560000 | tf_op jit(solution)/shard_map/pallas_call | solution.py:236
  44.1 2.4 %shard_map.77 = (f32[2,200,400]{2,1,0:T(8,128)S(1)}, f32[200,1600]{1,0:T(8,128)S(1)}) custom-call(f32[4]{0:T(128)S(1)} %copy-done, bf16[2,200,1600]{2,1,0:T(8,128)(2,1)S(1)} %get-tuple-element.19.refs_2_.chol_ref, bf16[1,200,1600]{2,1,0:T(8,128)(2,1)S(1)} %collective-permute-done.3.refs_0_, f32[2,200,400]{2,1,0:T(8,128)S(1)} %get-tuple-element.27.refs_1_, ...), custom_call_target="tpu_custom_call" | custom-call | flops 320000000 | bytes 1920000 | tf_op jit(solution)/shard_map/pallas_call | solution.py:236
  46.6 0.0 collective-permute-done.4.refs_0_
  46.6 3.4 %shard_map.78 = (f32[2,200,400]{2,1,0:T(8,128)}, f32[400,200]{1,0:T(8,128)}) custom-call(f32[4]{0:T(128)S(1)} %copy-done, bf16[2,200,1600]{2,1,0:T(8,128)(2,1)S(1)} %get-tuple-element.19.refs_2_.chol_ref, bf16[1,200,1600]{2,1,0:T(8,128)(2,1)S(1)} %collective-permute-done.4.refs_0_, f32[2,200,400]{2,1,0:T(8,128)S(1)} %get-tuple-element.29.refs_1_, ...), custom_call_target="tpu_custom_call" | custom-call | flops 576000000 | bytes 1920000 | tf_op jit(solution)/shard_map/pallas_call | solution.py:236
Async XLA Ops:
  0.6 21.7 %copy-start = (f32[4]{0:T(128)S(1)}, f32[4]{0:T(128)}, u32[]{:S(2)}) copy-start(f32[4]{0:T(128)} %cot_ref.5) | copy-start | bytes 52
  0.6 18.2 %collective-permute-start.3 = (bf16[1,200,1600]{2,1,0:T(8,128)(2,1)}, bf16[1,200,1600]{2,1,0:T(8,128)(2,1)S(1)}, u32[]{:S(2)}, u32[]{:S(2)}) collective-permute-start(bf16[1,200,1600]{2,1,0:T(8,128)(2,1)} %refs_1_.1), channel_id=1, source_target_pairs={{0,2},{1,3},{2,0},{3,1},{4,6},{5,7},{6,4},{7,5},{8,10},{9,11},{10,... | collective-permute-start | bytes 1920008 | tf_op jit(solution)/shard_map/ppermute | solution.py:285
  3.7 37.9 %collective-permute-start.5 = (bf16[1,200,1600]{2,1,0:T(8,128)(2,1)}, bf16[1,200,1600]{2,1,0:T(8,128)(2,1)S(1)}, u32[]{:S(2)}, u32[]{:S(2)}) collective-permute-start(bf16[1,200,1600]{2,1,0:T(8,128)(2,1)} %refs_1_.1), channel_id=1, source_target_pairs={{0,1},{1,0},{2,3},{3,2},{4,5},{5,4},{6,7},{7,6},{8,9},{9,8},{10,11... | collective-permute-start | bytes 1920008 | tf_op jit(solution)/shard_map/ppermute | solution.py:285
  18.8 27.7 %collective-permute-start.4 = (bf16[1,200,1600]{2,1,0:T(8,128)(2,1)S(1)}, bf16[1,200,1600]{2,1,0:T(8,128)(2,1)S(1)}, u32[]{:S(2)}, u32[]{:S(2)}) collective-permute-start(bf16[1,200,1600]{2,1,0:T(8,128)(2,1)S(1)} %collective-permute-done.3.refs_0_), channel_id=1, source_target_pairs={{0,1},{1,0},{2,3},{3,2},{4,5},{5,4},{6,7},{7,6},{8,9},{9,8},{10,11... | collective-permute-start | bytes 1920008 | tf_op jit(solution)/shard_map/ppermute | solution.py:285
  23.8 9.8 %collective-permute-start = (bf16[40,2000]{1,0:T(8,128)(2,1)S(1)}, bf16[40,2000]{1,0:T(8,128)(2,1)S(1)}, u32[]{:S(2)}, u32[]{:S(2)}) collective-permute-start(bf16[40,2000]{1,0:T(8,128)(2,1)S(1)} %get-tuple-element.23), channel_id=1, source_target_pairs={{0,4},{4,0},{8,12},{12,8},{1,5},{5,1},{9,13},{13,9},{2,6},{6,2},{1... | collective-permute-start | bytes 480008 | tf_op jit(solution)/shard_map/ppermute | solution.py:285
  25.6 15.0 %collective-permute-start.1 = (bf16[40,2000]{1,0:T(8,128)(2,1)S(1)}, bf16[40,2000]{1,0:T(8,128)(2,1)S(1)}, u32[]{:S(2)}, u32[]{:S(2)}) collective-permute-start(bf16[40,2000]{1,0:T(8,128)(2,1)S(1)} %get-tuple-element.24), channel_id=1, source_target_pairs={{0,8},{4,12},{8,0},{12,4},{1,9},{5,13},{9,1},{13,5},{2,10},{6,14},... | collective-permute-start | bytes 480008 | tf_op jit(solution)/shard_map/ppermute | solution.py:285
  28.2 12.5 %collective-permute-start.2 = (bf16[40,2000]{1,0:T(8,128)(2,1)S(1)}, bf16[40,2000]{1,0:T(8,128)(2,1)S(1)}, u32[]{:S(2)}, u32[]{:S(2)}) collective-permute-start(bf16[40,2000]{1,0:T(8,128)(2,1)S(1)} %get-tuple-element.25), channel_id=1, source_target_pairs={{0,12},{4,8},{8,4},{12,0},{1,13},{5,9},{9,5},{13,1},{2,14},{6,10},... | collective-permute-start | bytes 480008 | tf_op jit(solution)/shard_map/ppermute | solution.py:285
